TPU v7x, 32 devices: a whole 2x2x4 slice. The times are simulated.
32 devices in a mesh: gx: 8 (over y, x, core), gy: 4 (over z).
Axes of the slice: x: 2, y: 2, z: 4, core: 2. Of those that a mesh axis runs over, the one named last changes fastest.
Arguments:
- object_field: float32 [2, 8192, 4096], P(None, 'gx', 'gy'), may hold values from -5 to 5
- probe: float32 [2, 256, 256], replicated, may hold values from -5 to 5
- centers: int32 [512, 2], P(('gx', 'gy')), may hold values from 0 to 1023
- live: int32 [512], P(('gx', 'gy')), may hold values from 0 to 1, as said below
- measured: float32 [512, 256, 256], P(('gx', 'gy')), may hold values from 0.5 to 2.5
Outputs:
- object_grad: float32 [2, 8192, 4096], P(None, 'gx', 'gy')
- probe_grad: float32 [2, 256, 256], replicated
- slot_loss: float32 [512], P(('gx', 'gy'))
Inputs may be any that keep to these rules, and one draw needn't show every extreme that they name: In each tile's 16 slots the live ones come first; every tile has at least one live slot, and some tile has all 16 live.
All inputs are finite; a program needn't handle non-finite values.
Results may differ from a plain program's by a relative error of at most 0.0001.
Values sent between devices are 32-bit elements; how exact they have to be, the bound alone decides.
No kernel may reach another device: no remote copies, remote signals or barrier semaphores. Data moves between devices by JAX's collectives and lax.ppermute only.
A program may use at most 192 MiB of HBM per device.

v0:
```python
import math

import jax
import jax.numpy as jnp
from jax import lax
from jax.sharding import PartitionSpec as P


def with_halo(cells, sides, width):
    for axis, dim in sides:
        count = lax.axis_size(axis)
        ends = count - 1
        head = lax.slice_in_dim(cells, 0, width, axis=dim)
        tail = lax.slice_in_dim(cells, cells.shape[dim] - width, cells.shape[dim], axis=dim)
        cells = jnp.concatenate(
            [
                lax.ppermute(tail, axis, [(i, (i + 1) % count) for i in range(ends)]),
                cells,
                lax.ppermute(head, axis, [((i + 1) % count, i) for i in range(ends)]),
            ],
            axis=dim,
        )
    return cells


def dft_tables(extent):
    steps_k = jnp.arange(extent, dtype=jnp.int32)
    phase = (steps_k[:, None] * steps_k[None, :] % extent).astype(jnp.float32)
    angle = phase * (-2.0 * math.pi / extent)
    norm_c = 1.0 / math.sqrt(extent)
    return (jnp.cos(angle) * norm_c, jnp.sin(angle) * norm_c)


def product(left, right):
    return jnp.dot(left, right, precision=lax.Precision.HIGHEST, preferred_element_type=jnp.float32)


def transform(real_in, imag_in, cos_table, sin_table):
    left_re = product(cos_table, real_in) - product(sin_table, imag_in)
    left_im = product(cos_table, imag_in) + product(sin_table, real_in)
    out_re = product(left_re, cos_table) - product(left_im, sin_table)
    out_im = product(left_re, sin_table) + product(left_im, cos_table)
    return (out_re, out_im)


def fold_rows(padded, half_width):
    total = padded.shape[1]
    middle = padded[:, 2 * half_width : total - 2 * half_width]
    inner = middle.shape[1]
    middle = middle.at[:, :half_width].add(padded[:, :half_width])
    middle = middle.at[:, inner - half_width :].add(padded[:, total - half_width :])
    return middle


def fold_cols(padded, half_width):
    total = padded.shape[2]
    middle = padded[:, :, 2 * half_width : total - 2 * half_width]
    inner = middle.shape[2]
    middle = middle.at[:, :, :half_width].add(padded[:, :, :half_width])
    middle = middle.at[:, :, inner - half_width :].add(padded[:, :, total - half_width :])
    return middle


def on_device(object_field, probe, centers, live, measured):
    extent = probe.shape[1]
    half_width = extent // 2
    local_slots = centers.shape[0]
    row_ext = with_halo(object_field, (("gx", 1),), half_width)
    extended = with_halo(row_ext, (("gy", 2),), half_width)
    cos_table, sin_table = dft_tables(extent)
    back_sin = -sin_table
    probe_re = probe[0]
    probe_im = probe[1]

    def visit(slot_index, state_now):
        grad_ext, acc_re, acc_im, losses = state_now
        row_at = centers[slot_index, 0]
        col_at = centers[slot_index, 1]
        zero_at = jnp.zeros((), jnp.int32)
        patch_obj = lax.dynamic_slice(extended, (zero_at, row_at, col_at), (2, extent, extent))
        obj_re = patch_obj[0]
        obj_im = patch_obj[1]
        wave_re = probe_re * obj_re - probe_im * obj_im
        wave_im = probe_re * obj_im + probe_im * obj_re
        far_re, far_im = transform(wave_re, wave_im, cos_table, sin_table)
        modulus = jnp.sqrt(far_re * far_re + far_im * far_im + 1.0)
        differ = modulus - measured[slot_index]
        weight = live[slot_index].astype(jnp.float32)
        factor = differ / modulus * weight
        back_re, back_im = transform(far_re * factor, far_im * factor, cos_table, back_sin)
        grad_re = probe_re * back_re + probe_im * back_im
        grad_im = probe_re * back_im - probe_im * back_re
        old_patch = lax.dynamic_slice(grad_ext, (zero_at, row_at, col_at), (2, extent, extent))
        grad_ext = lax.dynamic_update_slice(
            grad_ext, old_patch + jnp.stack([grad_re, grad_im]), (zero_at, row_at, col_at)
        )
        acc_re = acc_re + obj_re * back_re + obj_im * back_im
        acc_im = acc_im + obj_re * back_im - obj_im * back_re
        loss = 0.5 * weight * jnp.sum(differ * differ) / (extent * extent)
        losses = losses.at[slot_index].set(loss)
        return (grad_ext, acc_re, acc_im, losses)

    start = (
        jnp.zeros(extended.shape, jnp.float32),
        jnp.zeros(probe_re.shape, jnp.float32),
        jnp.zeros(probe_re.shape, jnp.float32),
        jnp.zeros((local_slots,), jnp.float32),
    )
    final = lax.fori_loop(0, local_slots, visit, start)
    grad_ext, acc_re, acc_im, slot_loss = final
    col_pad = with_halo(grad_ext, (("gy", 2),), half_width)
    col_done = fold_cols(col_pad, half_width)
    row_pad = with_halo(col_done, (("gx", 1),), half_width)
    object_grad = fold_rows(row_pad, half_width)
    totals = lax.psum((acc_re, acc_im), ("gx", "gy"))
    slots_all = local_slots * lax.axis_size("gx") * lax.axis_size("gy")
    probe_grad = jnp.stack([totals[0], totals[1]]) / math.sqrt(slots_all)
    return (object_grad, probe_grad, slot_loss)


def solution(mesh):
    placed = (
        P(None, "gx", "gy"),
        P(),
        P(("gx", "gy"), None),
        P(("gx", "gy")),
        P(("gx", "gy"), None, None),
    )
    return jax.shard_map(
        on_device,
        mesh=mesh,
        in_specs=placed,
        out_specs=(P(None, "gx", "gy"), P(), P(("gx", "gy"))),
        check_vma=False,
    )
```

profile of v0, /device:TPU:0, one launch (start us, length us, event | category | flops | bytes accessed | tf_op | source)
XLA Modules:
  0.0 977.2 jit_solution(3645311747882526065)
XLA Ops:
  13.7 4.3 constant_dynamic-update-slice_fusion.1
  18.1 3.9 copy-done.1
  23.7 4.4 collective-permute-start.2
  29.5 14.0 %collective-permute-done.2 = f32[2,1280,128]{2,1,0:T(8,128)S(1)} collective-permute-done((f32[2,1280,128]{2,1,0:T(8,128)}, f32[2,1280,128]{2,1,0:T(8,128)S(1)}, u32[]{:S(2)}, u32[]{:S(2)}) %collective-permute-start.2) | collective-permute-done | bytes 1310752 | tf_op jit(solution)/shard_map/ppermute | solution.py:17
  43.4 4.5 collective-permute-done.3
  47.9 10.1 %pad_maximum_fusion = f32[2,1280,1280]{2,1,0:T(8,128)} fusion(f32[2,1280,128]{2,1,0:T(8,128)} %collective-permute-done.3, f32[2,1280,1024]{2,1,0:T(8,128)} %copy-done.1, f32[2,1280,128]{2,1,0:T(8,128)S(1)} %collective-permute-done.2), kind=kLoop, calls=%fused_computation.136 | loop fusion | flops 6553600 | bytes 26214400 | tf_op jit(solution)/shard_map/concatenate | solution.py:15
  58.0 5.6 broadcast_in_dim.8
  63.6 681.4 %while.26 = (s32[]{:T(128)}, f32[2,1280,1280]{2,1,0:T(8,128)}, f32[256,256]{1,0:T(8,128)S(1)}, f32[256,256]{1,0:T(8,128)S(1)}, f32[16]{0:T(128)S(1)}, /*index=5*...) while((s32[]{:T(128)}, f32[2,1280,1280]{2,1,0:T(8,128)}, ...), condition=%wide.region_2.3_spmd.clone.clone, body=%wide.region_0.2_spmd.clone.clone.sunk | while | flops 3240296448 | bytes 19137056 | solution.py:109
  81.1 3.1 multiply_reduce_fusion.2
  99.6 6.8 dynamic_update_slice.10
  123.8 3.1 multiply_reduce_fusion.2
  142.4 6.1 dynamic_update_slice.10
  165.9 3.1 multiply_reduce_fusion.2
  184.4 6.8 dynamic_update_slice.10
  208.7 3.1 multiply_reduce_fusion.2
  227.2 6.5 dynamic_update_slice.10
  251.1 3.1 multiply_reduce_fusion.2
  269.6 6.6 dynamic_update_slice.10
  293.7 3.1 multiply_reduce_fusion.2
  312.2 6.1 dynamic_update_slice.10
  335.7 3.1 multiply_reduce_fusion.2
  354.3 6.5 dynamic_update_slice.10
  378.2 3.1 multiply_reduce_fusion.2
  396.7 6.8 dynamic_update_slice.10
  421.0 3.1 multiply_reduce_fusion.2
  439.5 6.8 dynamic_update_slice.10
  463.7 3.1 multiply_reduce_fusion.2
  482.2 6.8 dynamic_update_slice.10
  506.5 3.1 multiply_reduce_fusion.2
  525.0 6.8 dynamic_update_slice.10
  549.2 3.1 multiply_reduce_fusion.2
  567.7 6.8 dynamic_update_slice.10
  591.9 3.1 multiply_reduce_fusion.2
  610.4 6.7 dynamic_update_slice.10
  634.5 3.1 multiply_reduce_fusion.2
  653.0 6.8 dynamic_update_slice.10
  695.7 6.8 dynamic_update_slice.10
  738.5 6.5 dynamic_update_slice.10
  745.1 3.2 fusion.113
  748.2 3.7 collective-permute-start.4
  753.2 5.1 slice.171
  758.3 7.9 collective-permute-done.4
  768.2 4.4 collective-permute-done.5
  774.3 4.0 copy-done
  779.7 18.4 %collective-permute-start.6 = (f32[2,128,1024]{2,1,0:T(8,128)}, f32[2,128,1024]{2,1,0:T(8,128)S(1)}, u32[]{:S(2)}, u32[]{:S(2)}) collective-permute-start(f32[2,128,1024]{2,1,0:T(8,128)} %get-tuple-element.478), channel_id=1, source_target_pairs={{0,4},{4,8},{8,12},{12,16},{16,20},{20,24},{24,28},{1,5},{5,9},{9,... | collective-permute-start | bytes 3145736 | tf_op jit(solution)/shard_map/ppermute | solution.py:17
  799.5 159.7 %all-reduce.3.cloned.1.call-done = (f32[1,256,256]{2,1,0:T(8,128)}, f32[1,256,256]{2,1,0:T(8,128)}) async-done(((f32[1,256,256]{2,1,0:T(8,128)}, f32[1,256,256]{2,1,0:T(8,128)}), (f32[1,256,256]{2,1,0:T(8,128)}, f32[1,256,256]{2,1,0:T(8,128)})) %all-reduce.3.cloned.1.call-update) | async-done | bytes 524304 | tf_op jit(solution)/shard_map/psum | solution.py:115
  961.1 4.2 slice.188
  967.0 3.4 copy-done.2
  (362 shorter events, 466.9 us)
Async XLA Ops:
  7.2 952.0 %all-reduce.3.cloned.1.call-start = ((), (), s32[]{:S(2)}) async-start(), calls=%async_computation | async-start | bytes 1048576 | tf_op jit(solution)/shard_map/psum | solution.py:115
  8.9 4.7 collective-permute-start
  11.4 6.6 collective-permute-start.1
  13.6 15.8 %copy-start.5 = (f32[2,256,256]{2,1,0:T(8,128)S(1)}, f32[2,256,256]{2,1,0:T(8,128)}, u32[]{:S(2)}) copy-start(f32[2,256,256]{2,1,0:T(8,128)} %param.18) | copy-start | bytes 1572868
  18.1 3.9 copy-start.1
  23.7 19.7 %collective-permute-start.2 = (f32[2,1280,128]{2,1,0:T(8,128)}, f32[2,1280,128]{2,1,0:T(8,128)S(1)}, u32[]{:S(2)}, u32[]{:S(2)}) collective-permute-start(f32[2,1280,128]{2,1,0:T(8,128)} %get-tuple-element.479), channel_id=1, source_target_pairs={{0,1},{1,2},{2,3},{4,5},{5,6},{6,7},{8,9},{9,10},{10,11},{12,13},{... | collective-permute-start | bytes 3932168 | tf_op jit(solution)/shard_map/ppermute | solution.py:17
  28.1 19.8 %collective-permute-start.3 = (f32[2,1280,128]{2,1,0:T(8,128)}, f32[2,1280,128]{2,1,0:T(8,128)}, u32[]{:S(2)}, u32[]{:S(2)}) collective-permute-start(f32[2,1280,128]{2,1,0:T(8,128)} %get-tuple-element.480), channel_id=1, source_target_pairs={{1,0},{2,1},{3,2},{5,4},{6,5},{7,6},{9,8},{10,9},{11,10},{13,12},{... | collective-permute-start | bytes 3932168 | tf_op jit(solution)/shard_map/ppermute | solution.py:19
  58.0 5.6 copy-start.6
  58.0 5.6 copy-start.8
  745.0 13.3 %copy-start.3 = (f32[256,256]{1,0:T(8,128)}, f32[256,256]{1,0:T(8,128)S(1)}, u32[]{:S(2)}) copy-start(f32[256,256]{1,0:T(8,128)S(1)} %get-tuple-element.346) | copy-start | bytes 786436
  745.0 13.3 %copy-start.4 = (f32[256,256]{1,0:T(8,128)}, f32[256,256]{1,0:T(8,128)S(1)}, u32[]{:S(2)}) copy-start(f32[256,256]{1,0:T(8,128)S(1)} %get-tuple-element.345) | copy-start | bytes 786436
  745.1 13.3 %copy-start.7 = (f32[16]{0:T(128)}, f32[16]{0:T(128)S(1)}, u32[]{:S(2)}) copy-start(f32[16]{0:T(128)S(1)} %get-tuple-element.343) | copy-start | bytes 196
  748.2 18.0 %collective-permute-start.4 = (f32[2,1280,128]{2,1,0:T(8,128)}, f32[2,1280,128]{2,1,0:T(8,128)}, u32[]{:S(2)}, u32[]{:S(2)}) collective-permute-start(f32[2,1280,128]{2,1,0:T(8,128)} %get-tuple-element.476), channel_id=1, source_target_pairs={{0,1},{1,2},{2,3},{4,5},{5,6},{6,7},{8,9},{9,10},{10,11},{12,13},{... | collective-permute-start | bytes 3932168 | tf_op jit(solution)/shard_map/ppermute | solution.py:17
  751.9 20.7 %collective-permute-start.5 = (f32[2,1280,128]{2,1,0:T(8,128)S(1)}, f32[2,1280,128]{2,1,0:T(8,128)}, u32[]{:S(2)}, u32[]{:S(2)}) collective-permute-start(f32[2,1280,128]{2,1,0:T(8,128)S(1)} %get-tuple-element.475), channel_id=1, source_target_pairs={{1,0},{2,1},{3,2},{5,4},{6,5},{7,6},{9,8},{10,9},{11,10},{13,12},{... | collective-permute-start | bytes 3932168 | tf_op jit(solution)/shard_map/ppermute | solution.py:19
  774.2 4.0 copy-start
  779.7 185.6 %collective-permute-start.6 = (f32[2,128,1024]{2,1,0:T(8,128)}, f32[2,128,1024]{2,1,0:T(8,128)S(1)}, u32[]{:S(2)}, u32[]{:S(2)}) collective-permute-start(f32[2,128,1024]{2,1,0:T(8,128)} %get-tuple-element.478), channel_id=1, source_target_pairs={{0,4},{4,8},{8,12},{12,16},{16,20},{20,24},{24,28},{1,5},{5,9},{9,... | collective-permute-start | bytes 3145736 | tf_op jit(solution)/shard_map/ppermute | solution.py:17
  798.2 168.5 %collective-permute-start.7 = (f32[2,128,1024]{2,1,0:T(8,128)}, f32[2,128,1024]{2,1,0:T(8,128)S(1)}, u32[]{:S(2)}, u32[]{:S(2)}) collective-permute-start(f32[2,128,1024]{2,1,0:T(8,128)} %get-tuple-element.477), channel_id=1, source_target_pairs={{4,0},{8,4},{12,8},{16,12},{20,16},{24,20},{28,24},{5,1},{9,5},{13... | collective-permute-start | bytes 3145736 | tf_op jit(solution)/shard_map/ppermute | solution.py:19
  967.0 3.4 copy-start.2
Sparse Core Ops, SparseCore 0:
  799.6 159.5 all-reduce.2
where the time goes:
time: 983 us; the launch traced here: 977 us
  matrix products  425 us (43%)
  waiting for transfers between devices  191 us (19%)
  local copies, waits for them, and re-layouts  164 us (17%)
  loops' own time  85.2 us (9%)
  other arithmetic  63.4 us (6%)
  starting transfers between devices  34.1 us (3%)
  between operations  14.3 us (1%)
    dot_general x256, matrix products, product(): jnp.dot(left, right, precision=lax.Precision.HIGHEST, preferred_element_t...  425 us
    psum x1, waiting for transfers between devices, on_device(): totals = lax.psum((acc_re, acc_im), ('gx', 'gy'))  160 us
    dynamic_update_slice x16, local copies, waits for them, and re-layouts, visit(): lax.dynamic_update_slice(grad_ext, old_patch + jnp.stack([grad_re, grad_i...  106 us
    another operation x1, loops' own time, on_device(): final = lax.fori_loop(0, local_slots, visit, start)  85.2 us
    ppermute x4, starting transfers between devices, with_halo(): lax.ppermute(tail, axis, [(i, (i + 1) % count) for i in range(ends)])  28.9 us
    ppermute x4, waiting for transfers between devices, with_halo(): lax.ppermute(tail, axis, [(i, (i + 1) % count) for i in range(ends)])  22.8 us
    add x16, other arithmetic, visit(): old_patch + jnp.stack([grad_re, grad_im])  21.9 us
    add x16, other arithmetic, visit(): wave_im = probe_re * obj_im + probe_im * obj_re  21.5 us
  transfers between devices with their start and end apart: 9, of which 6 were waited for; matrix products, arithmetic and copies ran while one was open for 2% of the time, Pallas kernels for 0%

commit v1 on v0

v1 whole, which is shorter than its diff:
```python
import functools
import math

import jax
import jax.numpy as jnp
import numpy as np
from jax import lax
from jax.experimental import pallas as pl
from jax.experimental.pallas import tpu as pltpu
from jax.sharding import PartitionSpec as P

LANES = 128
SUBS = 8
BF = jnp.bfloat16
F32 = jnp.float32


def split_np(table):
    hi = table.astype(np.float32).astype(jnp.bfloat16)
    lo = (table - hi.astype(np.float64)).astype(np.float32).astype(jnp.bfloat16)
    return hi, lo


def tables_np(extent):
    half = extent // 2
    k = np.arange(extent)[:, None]
    n = np.arange(half)[None, :]
    angle = -2.0 * np.pi * ((k * n) % extent) / extent
    re = np.cos(angle) / math.sqrt(extent)
    im = np.sin(angle) / math.sqrt(extent)
    lefts, rights = [], []
    for parity in range(2):
        a, b = re[parity::2], im[parity::2]
        left = np.block([[a, -b], [b, a]])
        for mat in (left, left.T):
            hi, lo = split_np(mat)
            lefts.append(np.concatenate([hi, lo, hi], axis=1))
            rights.append(np.concatenate([hi, lo, hi], axis=0))
    forward_rows = np.stack([lefts[0], lefts[2]])
    forward_cols = np.stack([rights[1], rights[3]])
    back_cols = np.stack([rights[0], rights[2]])
    back_rows = np.stack([lefts[1], lefts[3]])
    pick = np.zeros((extent, extent), np.float32)
    pick[2 * np.arange(half), np.arange(half)] = 1
    pick[2 * np.arange(half) + 1, half + np.arange(half)] = 1
    pick = np.concatenate([pick, pick], axis=0).astype(jnp.bfloat16)
    return forward_rows, forward_cols, back_cols, back_rows, pick


def parts(x):
    hi = x.astype(BF)
    lo = (x - hi.astype(F32)).astype(BF)
    return hi, lo


def matmul(a, b):
    return jnp.dot(a, b, preferred_element_type=F32)


def slot_kernel(
    phase, extent, slots, tile,
    centers, live, *refs,
):
    half = extent // 2
    inner = phase == "inner"
    it = iter(refs)
    take = lambda n: [next(it) for _ in range(n)]
    tile_hbm, probe, meas_hbm, fr, fc, bc, br, pick = take(8)
    if not inner:
        up_hbm, down_hbm, left_hbm, right_hbm, corner_hbm, grad_in, acc_in, loss_in = take(8)
    grad_out, acc_out, loss_out = take(3)
    if not inner:
        gup, gdown, gleft, gright = take(4)
    ext, grad, shifted, accs, turned, meas, sh_h, sh_l, sems, msems = take(10)
    size = tile + 2 * half
    mid = pl.ds(half, tile)

    loads = []

    def load(src, dst):
        loads.append(pltpu.make_async_copy(src, dst, sems.at[len(loads)]))
        loads[-1].start()

    load(tile_hbm, ext.at[:, mid, mid])
    if not inner:
        load(up_hbm, ext.at[:, pl.ds(0, half), mid])
        load(down_hbm, ext.at[:, pl.ds(half + tile, half), mid])
        load(left_hbm, ext.at[:, mid, pl.ds(0, half)])
        load(right_hbm, ext.at[:, mid, pl.ds(half + tile, half)])
        for i, rows in enumerate((0, half + tile)):
            for j, cols in enumerate((0, half + tile)):
                load(corner_hbm.at[j, i], ext.at[:, pl.ds(rows, half), pl.ds(cols, half)])
        load(grad_in, grad.at[:, mid, mid])
    fetches = [
        pltpu.make_async_copy(meas_hbm.at[:, :, pl.ds(j * LANES, LANES)], meas.at[j], msems.at[j])
        for j in range(2)
    ]
    for f in fetches:
        f.start()

    for p in range(2):
        plane = probe[p]
        for b in range(SUBS):
            shifted[b, p] = pltpu.roll(plane, b, 0) if b else plane
    accs[...] = jnp.zeros_like(accs)
    if inner:
        loss_out[...] = jnp.zeros_like(loss_out)
        zero_rows = jnp.zeros((2, SUBS, size), F32)

        def clear(i, c):
            grad[:, pl.ds(pl.multiple_of(i * SUBS, SUBS), SUBS), :] = zero_rows
            return c

        lax.fori_loop(0, size // SUBS, clear, 0)
    else:
        loss_out[...] = loss_in[...]
        edge = jnp.zeros((2, SUBS, size), F32)

        def clear_rows(i, c):
            at = pl.multiple_of(i * SUBS, SUBS)
            grad[:, pl.ds(at, SUBS), :] = edge
            grad[:, pl.ds(half + tile + at, SUBS), :] = edge
            return c

        lax.fori_loop(0, half // SUBS, clear_rows, 0)
        side = jnp.zeros((2, SUBS, half), F32)

        def clear_cols(i, c):
            at = pl.multiple_of(half + i * SUBS, SUBS)
            grad[:, pl.ds(at, SUBS), pl.ds(0, half)] = side
            grad[:, pl.ds(at, SUBS), pl.ds(half + tile, half)] = side
            return c

        lax.fori_loop(0, tile // SUBS, clear_cols, 0)
    for c in loads:
        c.wait()
    for f in fetches:
        f.wait()

    chunk = 32
    lane8 = lax.broadcasted_iota(jnp.int32, (SUBS, LANES), 1)
    sub8 = lax.broadcasted_iota(jnp.int32, (SUBS, LANES), 0)

    def visit(s):
        row = centers[s, 0]
        col = centers[s, 1]
        b = lax.rem(row, SUBS)
        r = lax.rem(col, LANES)
        a8 = pl.multiple_of(row - b, SUBS)
        q = pl.multiple_of(col - r, LANES)
        lane = lax.broadcasted_iota(jnp.int32, (chunk, LANES), 1)

        def at(off):
            return pl.ds(pl.multiple_of(a8 + off, SUBS), chunk)

        def at8(off):
            return pl.ds(pl.multiple_of(a8 + off, SUBS), SUBS)

        cols = [pl.ds(pl.multiple_of(q + j * LANES, LANES), LANES) for j in range(3)]

        def patch(p, i):
            c0 = jnp.where(lane >= r, ext[p, at(i), cols[0]], ext[p, at(i), cols[2]])
            c1 = ext[p, at(i), cols[1]]
            if i == 0:
                x0 = jnp.where(lane8 >= r, ext[p, at8(extent), cols[0]], ext[p, at8(extent), cols[2]])
                x1 = ext[p, at8(extent), cols[1]]
                c0 = jnp.concatenate([jnp.where(sub8 >= b, c0[:SUBS], x0), c0[SUBS:]], axis=0)
                c1 = jnp.concatenate([jnp.where(sub8 >= b, c1[:SUBS], x1), c1[SUBS:]], axis=0)
            return c0, c1

        def turn(p, i):
            r0 = pltpu.roll(shifted[b, p, i:i + chunk, :LANES], r, 1)
            r1 = pltpu.roll(shifted[b, p, i:i + chunk, LANES:], r, 1)
            return jnp.where(lane >= r, r0, r1), jnp.where(lane >= r, r1, r0)

        def wave(i):
            o_re, o_im = patch(0, i), patch(1, i)
            p_re, p_im = turn(0, i), turn(1, i)
            out = []
            for j in range(2):
                js = slice(j * LANES, (j + 1) * LANES)
                turned[0, i:i + chunk, js] = p_re[j]
                turned[1, i:i + chunk, js] = p_im[j]
                out.append((p_re[j] * o_re[j] - p_im[j] * o_im[j], p_re[j] * o_im[j] + p_im[j] * o_re[j]))
            return out

        for i in range(0, half, chunk):
            top, bot = wave(i), wave(i + half)
            for j in range(2):
                js = slice(j * LANES, (j + 1) * LANES)
                for c in range(2):
                    for e, v in enumerate((top[j][c] + bot[j][c], top[j][c] - bot[j][c])):
                        hi, lo = parts(v)
                        sh_h[e, c * half + i:c * half + i + chunk, js] = hi
                        sh_l[e, c * half + i:c * half + i + chunk, js] = lo
        mids = []
        for e in range(2):
            xh = sh_h[e]
            y = matmul(fr[e], jnp.concatenate([xh, xh, sh_l[e]], axis=0))
            mids.append((y[:half], y[half:]))
        far = []
        for sign in (1, -1):
            rows = []
            for re, im in mids:
                if sign == 1:
                    rows.append(jnp.concatenate([re[:, :half] + re[:, half:], im[:, :half] + im[:, half:]], axis=1))
                else:
                    rows.append(jnp.concatenate([re[:, :half] - re[:, half:], im[:, :half] - im[:, half:]], axis=1))
            x = jnp.concatenate(rows, axis=0)
            hi, lo = parts(x)
            far.append(matmul(jnp.concatenate([hi, hi, lo], axis=1), fc[0 if sign == 1 else 1]))
        m_rows = jnp.concatenate(
            [
                jnp.concatenate([meas[j, s, pl.ds(e, half, stride=2), :] for j in range(2)], axis=1)
                for e in range(2)
            ],
            axis=0,
        )
        m_hi, m_lo = parts(m_rows)
        amp = matmul(jnp.concatenate([m_hi, m_lo], axis=1), pick[...])
        total = jnp.zeros((SUBS, LANES), F32)
        backs = []
        for e in range(2):
            re, im = far[e][:, :half], far[e][:, half:]
            t = re * re + im * im + 1.0
            inv = lax.rsqrt(t)
            differ = t * inv - amp[:, e * half:(e + 1) * half]
            total = total + jnp.sum((differ * differ).reshape(extent // SUBS, SUBS, half), axis=0)
            factor = differ * inv
            z = jnp.concatenate([re * factor, im * factor], axis=1)
            hi, lo = parts(z)
            backs.append(matmul(jnp.concatenate([hi, hi, lo], axis=1), bc[e]))
        loss_out[s] = total
        left = backs[0] + backs[1]
        right = backs[0] - backs[1]
        outs = []
        for e in range(2):
            rs = slice(e * half, (e + 1) * half)
            x = jnp.concatenate(
                [
                    jnp.concatenate([left[rs, :half], right[rs, :half]], axis=1),
                    jnp.concatenate([left[rs, half:], right[rs, half:]], axis=1),
                ],
                axis=0,
            )
            hi, lo = parts(x)
            outs.append(matmul(br[e], jnp.concatenate([hi, hi, lo], axis=0)))
        for k, adj in enumerate((outs[0] + outs[1], outs[0] - outs[1])):
            for i0 in range(0, half, chunk):
                i = k * half + i0
                o_re, o_im = patch(0, i), patch(1, i)
                q_re, q_im = [], []
                for j in range(2):
                    js = slice(j * LANES, (j + 1) * LANES)
                    b_re = adj[i0:i0 + chunk, js]
                    b_im = adj[half + i0:half + i0 + chunk, js]
                    p_re, p_im = turned[0, i:i + chunk, js], turned[1, i:i + chunk, js]
                    g_re = p_re * b_re + p_im * b_im
                    g_im = p_re * b_im - p_im * b_re
                    q_re.append(o_re[j] * b_re + o_im[j] * b_im)
                    q_im.append(o_re[j] * b_im - o_im[j] * b_re)
                    for p, g in enumerate((g_re, g_im)):
                        if i == 0:
                            spill = jnp.where(sub8 < b, g[:SUBS], 0.0)
                            g = jnp.concatenate([jnp.where(sub8 >= b, g[:SUBS], 0.0), g[SUBS:]], axis=0)
                        if j == 0:
                            grad[p, at(i), cols[0]] += jnp.where(lane >= r, g, 0.0)
                            grad[p, at(i), cols[2]] += jnp.where(lane < r, g, 0.0)
                            if i == 0:
                                grad[p, at8(extent), cols[0]] += jnp.where(lane8 >= r, spill, 0.0)
                                grad[p, at8(extent), cols[2]] += jnp.where(lane8 < r, spill, 0.0)
                        else:
                            grad[p, at(i), cols[1]] += g
                            if i == 0:
                                grad[p, at8(extent), cols[1]] += spill
                back = lax.rem(LANES - r, LANES)
                for p, (h0, h1) in enumerate((q_re, q_im)):
                    h0 = pltpu.roll(h0, back, 1)
                    h1 = pltpu.roll(h1, back, 1)
                    keep = lane < LANES - r
                    accs[b, p, i:i + chunk, :LANES] += jnp.where(keep, h0, h1)
                    accs[b, p, i:i + chunk, LANES:] += jnp.where(keep, h1, h0)

    def step(s, c):
        row = centers[s, 0]
        col = centers[s, 1]
        inside = (row >= half) & (row <= tile - half) & (col >= half) & (col <= tile - half)
        wanted = inside if inner else jnp.logical_not(inside)

        @pl.when((live[s] > 0) & wanted)
        def _():
            visit(s)

        return c

    lax.fori_loop(0, slots, step, 0)

    stores = []

    def store(src, dst):
        stores.append(pltpu.make_async_copy(src, dst, sems.at[len(stores)]))
        stores[-1].start()

    if not inner:
        store(grad.at[:, :, pl.ds(0, half)], gleft)
        store(grad.at[:, :, pl.ds(half + tile, half)], gright)
        store(grad.at[:, pl.ds(0, half), mid], gup)
        store(grad.at[:, pl.ds(half + tile, half), mid], gdown)
    store(grad.at[:, mid, mid], grad_out)
    for p in range(2):
        acc = accs[0, p]
        for b in range(1, SUBS):
            acc = acc + pltpu.roll(accs[b, p], extent - b, 0)
        acc_out[p] = acc if inner else acc + acc_in[p]
    for c in stores:
        c.wait()


def run_slots(phase, centers, live, tile_obj, probe, measured, tables, extra=()):
    extent = probe.shape[1]
    half = extent // 2
    slots = centers.shape[0]
    tile = tile_obj.shape[1]
    size = tile + 2 * half
    inner = phase == "inner"
    smem = pl.BlockSpec(memory_space=pltpu.SMEM)
    hbm = pl.BlockSpec(memory_space=pl.ANY)
    vmem = pl.BlockSpec(memory_space=pltpu.VMEM)
    in_specs = [smem, smem, hbm, vmem, hbm] + [vmem] * 5
    out_shape = [
        jax.ShapeDtypeStruct((2, tile, tile), F32),
        jax.ShapeDtypeStruct((2, extent, extent), F32),
        jax.ShapeDtypeStruct((slots, SUBS, LANES), F32),
    ]
    out_specs = [hbm, vmem, vmem]
    if not inner:
        in_specs += [hbm] * 6 + [vmem, vmem]
        out_shape += [jax.ShapeDtypeStruct((2, half, tile), F32)] * 2
        out_shape += [jax.ShapeDtypeStruct((2, size, half), F32)] * 2
        out_specs += [hbm] * 4
    flops = slots * 16 * 2 * extent**3
    return pl.pallas_call(
        functools.partial(slot_kernel, phase, extent, slots, tile),
        out_shape=out_shape,
        in_specs=in_specs,
        out_specs=out_specs,
        scratch_shapes=[
            pltpu.VMEM((2, size, size), F32),
            pltpu.VMEM((2, size, size), F32),
            pltpu.VMEM((SUBS, 2, extent, extent), F32),
            pltpu.VMEM((SUBS, 2, extent, extent), F32),
            pltpu.VMEM((2, extent, extent), F32),
            pltpu.VMEM((2, slots, extent, LANES), F32),
            pltpu.VMEM((2, extent, extent), BF),
            pltpu.VMEM((2, extent, extent), BF),
            pltpu.SemaphoreType.DMA((12,)),
            pltpu.SemaphoreType.DMA((2,)),
        ],
        compiler_params=pltpu.CompilerParams(vmem_limit_bytes=60 * 2**20),
        cost_estimate=pl.CostEstimate(flops=flops, bytes_accessed=32 * 2**20, transcendentals=0),
        name="slots_" + phase,
    )(centers, live, tile_obj, probe, measured, *tables, *extra)


def shift(x, axis, up):
    n = lax.axis_size(axis)
    if up:
        return lax.ppermute(x, axis, [(i, i + 1) for i in range(n - 1)])
    return lax.ppermute(x, axis, [(i + 1, i) for i in range(n - 1)])


def sum_all(x, axes):
    flat = x.reshape(-1, LANES)

    def scatter(y, axis):
        n = lax.axis_size(axis)
        me = lax.axis_index(axis)
        rows = y.shape[0] // n
        own = lax.dynamic_slice_in_dim(y, me * rows, rows, 0)
        got = []
        for k in range(1, n):
            piece = lax.dynamic_slice_in_dim(y, lax.rem(me + k, n) * rows, rows, 0)
            got.append(lax.ppermute(piece, axis, [(i, (i + k) % n) for i in range(n)]))
        for piece in got:
            own = own + piece
        return own

    def gather(y, axis):
        n = lax.axis_size(axis)
        me = lax.axis_index(axis)
        rows = y.shape[0]
        out = jnp.zeros((n * rows,) + y.shape[1:], y.dtype)
        out = lax.dynamic_update_slice_in_dim(out, y, me * rows, 0)
        for k in range(1, n):
            piece = lax.ppermute(y, axis, [(i, (i + k) % n) for i in range(n)])
            out = lax.dynamic_update_slice_in_dim(out, piece, lax.rem(me + n - k, n) * rows, 0)
        return out

    for axis in axes:
        flat = scatter(flat, axis)
    for axis in reversed(axes):
        flat = gather(flat, axis)
    return flat.reshape(x.shape)


def on_device(object_field, probe, centers, live, measured):
    extent = probe.shape[1]
    half = extent // 2
    tile = object_field.shape[1]
    slots = centers.shape[0]
    tables = [jnp.asarray(t) for t in tables_np(extent)]

    up = shift(object_field[:, tile - half:, :], "gx", True)
    down = shift(object_field[:, :half, :], "gx", False)
    left = shift(object_field[:, :, tile - half:], "gy", True)
    right = shift(object_field[:, :, :half], "gy", False)
    ends = jnp.stack([up, down])
    corner_l = shift(ends[:, :, :, tile - half:], "gy", True)
    corner_r = shift(ends[:, :, :, :half], "gy", False)
    corners = jnp.stack([corner_l, corner_r])

    grad_a, acc_a, loss_a = run_slots("inner", centers, live, object_field, probe, measured, tables)
    grad_b, acc_b, loss_b, gup, gdown, gleft, gright = run_slots(
        "outer", centers, live, object_field, probe, measured, tables,
        (up, down, left, right, corners, grad_a, acc_a, loss_a),
    )
    from_left = shift(gright, "gy", True)
    from_right = shift(gleft, "gy", False)
    from_up = shift(gdown, "gx", True)
    from_down = shift(gup, "gx", False)
    bottoms = jnp.stack([from_left[:, half + tile:, :], from_right[:, half + tile:, :]])
    tops = jnp.stack([from_left[:, :half, :], from_right[:, :half, :]])
    corner_up = shift(bottoms, "gx", True)
    corner_down = shift(tops, "gx", False)
    totals = sum_all(acc_b, ("gx", "gy"))

    top_add = from_up.at[:, :, :half].add(corner_up[0]).at[:, :, tile - half:].add(corner_up[1])
    bot_add = from_down.at[:, :, :half].add(corner_down[0]).at[:, :, tile - half:].add(corner_down[1])
    out = grad_b
    out = out.at[:, :, :half].add(from_left[:, half:half + tile, :])
    out = out.at[:, :, tile - half:].add(from_right[:, half:half + tile, :])
    out = out.at[:, :half, :].add(top_add)
    out = out.at[:, tile - half:, :].add(bot_add)

    slots_all = slots * lax.axis_size("gx") * lax.axis_size("gy")
    probe_grad = totals / math.sqrt(slots_all)
    slot_loss = jnp.sum(loss_b, axis=(1, 2)) * (0.5 / (extent * extent))
    return out, probe_grad, slot_loss


def solution(mesh):
    placed = (
        P(None, "gx", "gy"),
        P(),
        P(("gx", "gy"), None),
        P(("gx", "gy")),
        P(("gx", "gy"), None, None),
    )
    return jax.shard_map(
        on_device,
        mesh=mesh,
        in_specs=placed,
        out_specs=(P(None, "gx", "gy"), P(), P(("gx", "gy"))),
        check_vma=False,
    )
```

time: 983 us -> 209 us (0.21)
  matrix products: 425 us -> 0 us
  local copies, waits for them, and re-layouts: 164 us -> 10.7 us
  waiting for transfers between devices: 191 us -> 63.6 us
  loops' own time: 85.2 us -> 0 us
  Pallas kernels: 0 us -> 60.7 us
  other arithmetic: 63.4 us -> 14.4 us
  starting transfers between devices: 34.1 us -> 56.9 us
  between operations: 14.3 us -> 1.02 us
    dot_general x256 -> x0, matrix products: 425 us -> none  [product(): jnp.dot(left, right, precision=lax.Precision.HIGHEST, preferred_element_t...]
    psum x1 -> x0, waiting for transfers between devices: 160 us -> none  [on_device(): totals = lax.psum((acc_re, acc_im), ('gx', 'gy'))]
    dynamic_update_slice x16 -> x11, local copies, waits for them, and re-layouts: 106 us -> 0.08 us  [the longest x10 0.06 us: gather(): lax.dynamic_update_slice_in_dim(out, piece, lax.rem(me + n - k, n) * rows...]
    another operation x1 -> x0, loops' own time: 85.2 us -> none  [on_device(): final = lax.fori_loop(0, local_slots, visit, start)]
    pallas_call x0 -> x2, Pallas kernels: none -> 60.7 us  [run_slots(): pl.pallas_call(functools.partial(slot_kernel, phase, extent, slots, tile)...]
    add x32 -> x1, other arithmetic: 43.4 us -> 0.03 us  [scatter(): own = own + piece]
    ppermute x8 -> x32, waiting for transfers between devices: 31.7 us -> 63.6 us  [the longest x10 58.8 us: gather(): piece = lax.ppermute(y, axis, [(i, (i + k) % n) for i in range(n)])]
    ppermute x8 -> x32, starting transfers between devices: 34.1 us -> 56.9 us  [the longest x10 24.1 us: scatter(): got.append(lax.ppermute(piece, axis, [(i, (i + k) % n) for i in range(n)]))]
  transfers between devices with their start and end apart: 9 -> 32, of which waited for: 6 -> 14; matrix products, arithmetic and copies ran while one was open for 2% -> 9% of each run, Pallas kernels for 0% -> 14%
where the time goes in v1:
time: 209 us; the launch traced here: 207 us
  waiting for transfers between devices  63.6 us (30%)
  Pallas kernels  60.7 us (29%)
  starting transfers between devices  56.9 us (27%)
  other arithmetic  14.4 us (7%)
  local copies, waits for them, and re-layouts  10.7 us (5%)
    pallas_call x2, Pallas kernels, run_slots(): pl.pallas_call(functools.partial(slot_kernel, phase, extent, slots, tile)...  60.7 us
    ppermute x10, waiting for transfers between devices, gather(): piece = lax.ppermute(y, axis, [(i, (i + k) % n) for i in range(n)])  58.8 us
    ppermute x10, starting transfers between devices, scatter(): got.append(lax.ppermute(piece, axis, [(i, (i + k) % n) for i in range(n)]))  24.1 us
    ppermute x6, starting transfers between devices, shift(): return lax.ppermute(x, axis, [(i, i + 1) for i in range(n - 1)])  21.5 us
    ppermute x6, starting transfers between devices, shift(): return lax.ppermute(x, axis, [(i + 1, i) for i in range(n - 1)])  7.72 us
    ppermute x10, waiting for transfers between devices, scatter(): got.append(lax.ppermute(piece, axis, [(i, (i + k) % n) for i in range(n)]))  4.82 us
  transfers between devices with their start and end apart: 32, of which 14 were waited for; matrix products, arithmetic and copies ran while one was open for 9% of the time, Pallas kernels for 14%

profile of v1, /device:TPU:0, one launch (start us, length us, event | category | flops | bytes accessed | tf_op | source)
XLA Modules:
  0.0 207.3 jit_solution(13541442841719247231)
XLA Ops:
  0.6 3.1 %fusion.13 = (f32[2,128,1024]{2,1,0:T(8,128)}, f32[2,128,1024]{2,1,0:T(8,128)}) fusion(f32[2,1024,1024]{2,1,0:T(8,128)} %refs_0_.3), kind=kLoop, calls=%fused_computation.56 | loop fusion | bytes 4194304 | tf_op jit(solution)/shard_map/slice | solution.py:414
  3.8 2.5 %collective-permute-start = (f32[2,128,1024]{2,1,0:T(8,128)}, f32[2,128,1024]{2,1,0:T(8,128)S(1)}, u32[]{:S(2)}, u32[]{:S(2)}) collective-permute-start(f32[2,128,1024]{2,1,0:T(8,128)} %get-tuple-element.124), channel_id=1, source_target_pairs={{0,4},{4,8},{8,12},{12,16},{16,20},{20,24},{24,28},{1,5},{5,9},{9,... | collective-permute-start | bytes 3145736 | tf_op jit(solution)/shard_map/ppermute | solution.py:368
  6.2 1.3 collective-permute-start.1
  7.5 2.7 %fusion.12 = (f32[2,1024,128]{2,1,0:T(8,128)S(1)}, f32[2,1024,128]{2,1,0:T(8,128)}) fusion(f32[2,1024,1024]{2,1,0:T(8,128)} %refs_0_.3), kind=kLoop, calls=%fused_computation.55 | loop fusion | bytes 4194304 | tf_op jit(solution)/shard_map/slice | solution.py:416
  10.2 5.3 %collective-permute-start.2 = (f32[2,1024,128]{2,1,0:T(8,128)}, f32[2,1024,128]{2,1,0:T(8,128)}, u32[]{:S(2)}, u32[]{:S(2)}) collective-permute-start(f32[2,1024,128]{2,1,0:T(8,128)} %get-tuple-element.122), channel_id=1, source_target_pairs={{0,1},{1,2},{2,3},{4,5},{5,6},{6,7},{8,9},{9,10},{10,11},{12,13},{... | collective-permute-start | bytes 3145736 | tf_op jit(solution)/shard_map/ppermute | solution.py:368
  15.5 1.3 collective-permute-start.3
  17.5 0.8 pad_maximum_fusion.2
  18.3 1.3 collective-permute-start.5
  19.6 5.9 %collective-permute-start.4 = (f32[2,2,128,128]{3,2,1,0:T(8,128)S(1)}, f32[2,2,128,128]{3,2,1,0:T(8,128)}, u32[]{:S(2)}, u32[]{:S(2)}) collective-permute-start(f32[2,2,128,128]{3,2,1,0:T(8,128)S(1)} %get-tuple-element.125), channel_id=1, source_target_pairs={{0,1},{1,2},{2,3},{4,5},{5,6},{6,7},{8,9},{9,10},{10,11},{12,13},{... | collective-permute-start | bytes 786440 | tf_op jit(solution)/shard_map/ppermute | solution.py:368
  25.5 29.6 %slots_inner.1 = (f32[2,1024,1024]{2,1,0:T(8,128)}, f32[2,256,256]{2,1,0:T(8,128)}, f32[16,8,128]{2,1,0:T(8,128)}) custom-call(s32[16,2]{1,0:T(8,128)} %copy.14.centers, s32[16]{0:T(128)} %live.3, f32[2,1024,1024]{2,1,0:T(8,128)} %refs_0_.3, f32[2,256,256]{2,1,0:T(8,128)} %refs_1_.3, f32[16,256,256]{2,1,0:T(8,128)} %refs_2_.3, ...), custom_call_target="tpu_custom_call" | custom-call | flops 8589934592 | bytes 33554432 | tf_op jit(solution)/shard_map/slots_inner/pallas_call | solution.py:342
  55.3 1.9 pad_maximum_fusion.refs_12_
  57.1 31.1 %slots_outer.1 = (f32[2,1024,1024]{2,1,0:T(8,128)}, f32[2,256,256]{2,1,0:T(8,128)}, f32[16,8,128]{2,1,0:T(8,128)}, f32[2,128,1024]{2,1,0:T(8,128)}, f32[2,128,10...) custom-call(s32[16,2]{1,0:T(8,128)} %copy.14.centers, s32[16]{0:T(128)} %live.3, ...), custom_call_target="tpu_custom_call" | custom-call | flops 8589934592 | bytes 33554432 | tf_op jit(solution)/shard_map/slots_outer/pallas_call | solution.py:342
  88.2 1.1 reshape.261
  89.4 10.1 %collective-permute-start.17 = (f32[128,128]{1,0:T(8,128)S(1)}, f32[128,128]{1,0:T(8,128)S(1)}, u32[]{:S(2)}, u32[]{:S(2)}) collective-permute-start(f32[128,128]{1,0:T(8,128)S(1)} %get-tuple-element.133), channel_id=1, source_target_pairs={{0,24},{4,28},{8,0},{12,4},{16,8},{20,12},{24,16},{28,20},{1,25},{... | collective-permute-start | bytes 196616 | tf_op jit(solution)/shard_map/ppermute | solution.py:383
  99.6 1.7 collective-permute-start.14
  101.3 1.2 collective-permute-start.13
  102.5 0.7 collective-permute-done.16
  103.3 1.8 collective-permute-done.15
  105.1 1.7 collective-permute-done.13
  107.4 1.3 collective-permute-start.21
  108.7 7.7 %collective-permute-start.20 = (f32[32,128]{1,0:T(8,128)S(1)}, f32[32,128]{1,0:T(8,128)S(1)}, u32[]{:S(2)}, u32[]{:S(2)}) collective-permute-start(f32[32,128]{1,0:T(8,128)S(1)} %get-tuple-element.140), channel_id=1, source_target_pairs={{0,2},{1,3},{2,0},{3,1},{4,6},{5,7},{6,4},{7,5},{8,10},{9,11},{10,... | collective-permute-start | bytes 49160 | tf_op jit(solution)/shard_map/ppermute | solution.py:383
  116.4 1.9 collective-permute-start.19
  118.3 3.0 %collective-permute-start.6 = (f32[2,1280,128]{2,1,0:T(8,128)}, f32[2,1280,128]{2,1,0:T(8,128)}, u32[]{:S(2)}, u32[]{:S(2)}) collective-permute-start(f32[2,1280,128]{2,1,0:T(8,128)} %get-tuple-element.113), channel_id=1, source_target_pairs={{0,1},{1,2},{2,3},{4,5},{5,6},{6,7},{8,9},{9,10},{10,11},{12,13},{... | collective-permute-start | bytes 3932168 | tf_op jit(solution)/shard_map/ppermute | solution.py:368
  121.3 1.3 collective-permute-start.7
  122.6 1.0 reduce_sum.9
  123.6 1.3 collective-permute-start.8
  125.0 1.3 collective-permute-start.10
  126.4 2.7 %collective-permute-start.22 = (f32[32,128]{1,0:T(8,128)S(1)}, f32[32,128]{1,0:T(8,128)S(1)}, u32[]{:S(2)}, u32[]{:S(2)}) collective-permute-start(f32[32,128]{1,0:T(8,128)S(1)} %get-tuple-element.120), channel_id=1, source_target_pairs={{0,1},{1,2},{2,3},{3,0},{4,5},{5,6},{6,7},{7,4},{8,9},{9,10},{10,1... | collective-permute-start | bytes 49160 | tf_op jit(solution)/shard_map/ppermute | solution.py:395
  129.6 23.9 %collective-permute-done.22 = f32[32,128]{1,0:T(8,128)S(1)} collective-permute-done((f32[32,128]{1,0:T(8,128)S(1)}, f32[32,128]{1,0:T(8,128)S(1)}, u32[]{:S(2)}, u32[]{:S(2)}) %collective-permute-start.22) | collective-permute-done | bytes 16416 | tf_op jit(solution)/shard_map/ppermute | solution.py:395
  153.5 4.6 %collective-permute-done.23 = f32[32,128]{1,0:T(8,128)S(1)} collective-permute-done((f32[32,128]{1,0:T(8,128)S(1)}, f32[32,128]{1,0:T(8,128)S(1)}, u32[]{:S(2)}, u32[]{:S(2)}) %collective-permute-start.23) | collective-permute-done | bytes 16416 | tf_op jit(solution)/shard_map/ppermute | solution.py:395
  158.1 3.7 %collective-permute-done.24 = f32[32,128]{1,0:T(8,128)S(1)} collective-permute-done((f32[32,128]{1,0:T(8,128)S(1)}, f32[32,128]{1,0:T(8,128)S(1)}, u32[]{:S(2)}, u32[]{:S(2)}) %collective-permute-start.24) | collective-permute-done | bytes 16416 | tf_op jit(solution)/shard_map/ppermute | solution.py:395
  161.9 4.5 %collective-permute-done.25 = f32[128,128]{1,0:T(8,128)S(1)} collective-permute-done((f32[128,128]{1,0:T(8,128)S(1)}, f32[128,128]{1,0:T(8,128)S(1)}, u32[]{:S(2)}, u32[]{:S(2)}) %collective-permute-start.25) | collective-permute-done | bytes 65568 | tf_op jit(solution)/shard_map/ppermute | solution.py:395
  166.4 5.1 %collective-permute-done.26 = f32[128,128]{1,0:T(8,128)S(1)} collective-permute-done((f32[128,128]{1,0:T(8,128)S(1)}, f32[128,128]{1,0:T(8,128)S(1)}, u32[]{:S(2)}, u32[]{:S(2)}) %collective-permute-start.26) | collective-permute-done | bytes 65568 | tf_op jit(solution)/shard_map/ppermute | solution.py:395
  171.6 3.7 %collective-permute-done.27 = f32[128,128]{1,0:T(8,128)S(1)} collective-permute-done((f32[128,128]{1,0:T(8,128)S(1)}, f32[128,128]{1,0:T(8,128)S(1)}, u32[]{:S(2)}, u32[]{:S(2)}) %collective-permute-start.27) | collective-permute-done | bytes 65568 | tf_op jit(solution)/shard_map/ppermute | solution.py:395
  175.4 4.1 %collective-permute-done.28 = f32[128,128]{1,0:T(8,128)S(1)} collective-permute-done((f32[128,128]{1,0:T(8,128)S(1)}, f32[128,128]{1,0:T(8,128)S(1)}, u32[]{:S(2)}, u32[]{:S(2)}) %collective-permute-start.28) | collective-permute-done | bytes 65568 | tf_op jit(solution)/shard_map/ppermute | solution.py:395
  179.6 3.7 %collective-permute-done.29 = f32[128,128]{1,0:T(8,128)S(1)} collective-permute-done((f32[128,128]{1,0:T(8,128)S(1)}, f32[128,128]{1,0:T(8,128)S(1)}, u32[]{:S(2)}, u32[]{:S(2)}) %collective-permute-start.29) | collective-permute-done | bytes 65568 | tf_op jit(solution)/shard_map/ppermute | solution.py:395
  183.2 0.7 collective-permute-start.30
  184.0 3.5 %collective-permute-done.30 = f32[128,128]{1,0:T(8,128)S(1)} collective-permute-done((f32[128,128]{1,0:T(8,128)S(1)}, f32[128,128]{1,0:T(8,128)S(1)}, u32[]{:S(2)}, u32[]{:S(2)}) %collective-permute-start.30) | collective-permute-done | bytes 65568 | tf_op jit(solution)/shard_map/ppermute | solution.py:395
  187.5 1.9 collective-permute-done.31
  189.5 0.9 div.10
  190.4 1.0 slice_bitcast_fusion.2
  191.4 1.0 slice_bitcast_fusion.3
  192.4 3.5 %collective-permute-start.9 = (f32[2,2,128,128]{3,2,1,0:T(8,128)S(1)}, f32[2,2,128,128]{3,2,1,0:T(8,128)S(1)}, u32[]{:S(2)}, u32[]{:S(2)}) collective-permute-start(f32[2,2,128,128]{3,2,1,0:T(8,128)S(1)} %pad_maximum_fusion.3), channel_id=1, source_target_pairs={{0,4},{4,8},{8,12},{12,16},{16,20},{20,24},{24,28},{1,5},{5,9},{9,... | collective-permute-start | bytes 786440 | tf_op jit(solution)/shard_map/ppermute | solution.py:368
  195.9 1.3 collective-permute-start.11
  197.2 2.6 %fusion.3 = f32[2,1024,1024]{2,1,0:T(8,128)} fusion(f32[2,1024,1024]{2,1,0:T(8,128)} %get-tuple-element.112, f32[2,1280,128]{2,1,0:T(8,128)} %collective-permute-done.6), kind=kLoop, calls=%fused_computation.7 | loop fusion | flops 262144 | bytes 3145728 | tf_op jit(solution)/shard_map/scatter-add | solution.py:440
  199.9 2.6 %fusion.2 = f32[2,1024,1024]{2,1,0:T(8,128)} fusion(f32[2,1024,1024]{2,1,0:T(8,128)} %fusion.3, f32[2,1280,128]{2,1,0:T(8,128)} %collective-permute-done.7), kind=kLoop, calls=%fused_computation.5 | loop fusion | flops 262144 | bytes 3145728 | tf_op jit(solution)/shard_map/scatter-add | solution.py:441
  202.6 2.3 %fusion.1 = f32[2,1024,1024]{2,1,0:T(8,128)} fusion(f32[2,1024,1024]{2,1,0:T(8,128)} %fusion.2, f32[2,128,1024]{2,1,0:T(8,128)S(1)} %fusion.9), kind=kLoop, calls=%fused_computation.3 | loop fusion | flops 262144 | bytes 3145728 | tf_op jit(solution)/shard_map/scatter-add | solution.py:442
  205.0 2.3 %fusion = f32[2,1024,1024]{2,1,0:T(8,128)} fusion(f32[2,1024,1024]{2,1,0:T(8,128)} %fusion.1, f32[2,128,1024]{2,1,0:T(8,128)S(1)} %fusion.5), kind=kLoop, calls=%fused_computation.1 | loop fusion | flops 262144 | bytes 3145728 | tf_op jit(solution)/shard_map/scatter-add | solution.py:443
  (63 shorter events, 2.4 us)
Async XLA Ops:
  0.6 16.2 %copy-start.2 = (s32[16,2]{0,1:T(2,128)S(1)}, s32[16,2]{0,1:T(2,128)}, u32[]{:S(2)}) copy-start(s32[16,2]{0,1:T(2,128)} %param.28) | copy-start | bytes 388
  3.8 13.7 %collective-permute-start = (f32[2,128,1024]{2,1,0:T(8,128)}, f32[2,128,1024]{2,1,0:T(8,128)S(1)}, u32[]{:S(2)}, u32[]{:S(2)}) collective-permute-start(f32[2,128,1024]{2,1,0:T(8,128)} %get-tuple-element.124), channel_id=1, source_target_pairs={{0,4},{4,8},{8,12},{12,16},{16,20},{20,24},{24,28},{1,5},{5,9},{9,... | collective-permute-start | bytes 3145736 | tf_op jit(solution)/shard_map/ppermute | solution.py:368
  6.2 11.3 %collective-permute-start.1 = (f32[2,128,1024]{2,1,0:T(8,128)}, f32[2,128,1024]{2,1,0:T(8,128)S(1)}, u32[]{:S(2)}, u32[]{:S(2)}) collective-permute-start(f32[2,128,1024]{2,1,0:T(8,128)} %get-tuple-element.123), channel_id=1, source_target_pairs={{4,0},{8,4},{12,8},{16,12},{20,16},{24,20},{28,24},{5,1},{9,5},{13... | collective-permute-start | bytes 3145736 | tf_op jit(solution)/shard_map/ppermute | solution.py:369
  10.2 46.9 %collective-permute-start.2 = (f32[2,1024,128]{2,1,0:T(8,128)}, f32[2,1024,128]{2,1,0:T(8,128)}, u32[]{:S(2)}, u32[]{:S(2)}) collective-permute-start(f32[2,1024,128]{2,1,0:T(8,128)} %get-tuple-element.122), channel_id=1, source_target_pairs={{0,1},{1,2},{2,3},{4,5},{5,6},{6,7},{8,9},{9,10},{10,11},{12,13},{... | collective-permute-start | bytes 3145736 | tf_op jit(solution)/shard_map/ppermute | solution.py:368
  15.5 41.6 %collective-permute-start.3 = (f32[2,1024,128]{2,1,0:T(8,128)S(1)}, f32[2,1024,128]{2,1,0:T(8,128)}, u32[]{:S(2)}, u32[]{:S(2)}) collective-permute-start(f32[2,1024,128]{2,1,0:T(8,128)S(1)} %get-tuple-element.121), channel_id=1, source_target_pairs={{1,0},{2,1},{3,2},{5,4},{6,5},{7,6},{9,8},{10,9},{11,10},{13,12},{... | collective-permute-start | bytes 3145736 | tf_op jit(solution)/shard_map/ppermute | solution.py:369
  17.5 37.7 %copy-start = (f32[2,128,1024]{2,1,0:T(8,128)}, f32[2,128,1024]{2,1,0:T(8,128)S(1)}, u32[]{:S(2)}) copy-start(f32[2,128,1024]{2,1,0:T(8,128)S(1)} %collective-permute-done.refs_8_) | copy-start | bytes 3145732
  17.5 37.7 %copy-start.1 = (f32[2,128,1024]{2,1,0:T(8,128)}, f32[2,128,1024]{2,1,0:T(8,128)S(1)}, u32[]{:S(2)}) copy-start(f32[2,128,1024]{2,1,0:T(8,128)S(1)} %collective-permute-done.1.refs_9_) | copy-start | bytes 3145732
  18.3 36.9 %collective-permute-start.5 = (f32[2,2,128,128]{3,2,1,0:T(8,128)}, f32[2,2,128,128]{3,2,1,0:T(8,128)}, u32[]{:S(2)}, u32[]{:S(2)}) collective-permute-start(f32[2,2,128,128]{3,2,1,0:T(8,128)} %get-tuple-element.126), channel_id=1, source_target_pairs={{1,0},{2,1},{3,2},{5,4},{6,5},{7,6},{9,8},{10,9},{11,10},{13,12},{... | collective-permute-start | bytes 786440 | tf_op jit(solution)/shard_map/ppermute | solution.py:369
  19.6 35.6 %collective-permute-start.4 = (f32[2,2,128,128]{3,2,1,0:T(8,128)S(1)}, f32[2,2,128,128]{3,2,1,0:T(8,128)}, u32[]{:S(2)}, u32[]{:S(2)}) collective-permute-start(f32[2,2,128,128]{3,2,1,0:T(8,128)S(1)} %get-tuple-element.125), channel_id=1, source_target_pairs={{0,1},{1,2},{2,3},{4,5},{5,6},{6,7},{8,9},{9,10},{10,11},{12,13},{... | collective-permute-start | bytes 786440 | tf_op jit(solution)/shard_map/ppermute | solution.py:368
  89.3 12.0 %collective-permute-start.18 = (f32[128,128]{1,0:T(8,128)S(1)}, f32[128,128]{1,0:T(8,128)S(1)}, u32[]{:S(2)}, u32[]{:S(2)}) collective-permute-start(f32[128,128]{1,0:T(8,128)S(1)} %get-tuple-element.132), channel_id=1, source_target_pairs={{0,28},{4,0},{8,4},{12,8},{16,12},{20,16},{24,20},{28,24},{1,29},{... | collective-permute-start | bytes 196616 | tf_op jit(solution)/shard_map/ppermute | solution.py:383
  89.4 13.1 %collective-permute-start.17 = (f32[128,128]{1,0:T(8,128)S(1)}, f32[128,128]{1,0:T(8,128)S(1)}, u32[]{:S(2)}, u32[]{:S(2)}) collective-permute-start(f32[128,128]{1,0:T(8,128)S(1)} %get-tuple-element.133), channel_id=1, source_target_pairs={{0,24},{4,28},{8,0},{12,4},{16,8},{20,12},{24,16},{28,20},{1,25},{... | collective-permute-start | bytes 196616 | tf_op jit(solution)/shard_map/ppermute | solution.py:383
  99.6 3.7 %collective-permute-start.16 = (f32[128,128]{1,0:T(8,128)S(1)}, f32[128,128]{1,0:T(8,128)S(1)}, u32[]{:S(2)}, u32[]{:S(2)}) collective-permute-start(f32[128,128]{1,0:T(8,128)S(1)} %get-tuple-element.134), channel_id=1, source_target_pairs={{0,20},{4,24},{8,28},{12,0},{16,4},{20,8},{24,12},{28,16},{1,21},{... | collective-permute-start | bytes 196616 | tf_op jit(solution)/shard_map/ppermute | solution.py:383
  99.6 5.5 %collective-permute-start.15 = (f32[128,128]{1,0:T(8,128)S(1)}, f32[128,128]{1,0:T(8,128)S(1)}, u32[]{:S(2)}, u32[]{:S(2)}) collective-permute-start(f32[128,128]{1,0:T(8,128)S(1)} %get-tuple-element.135), channel_id=1, source_target_pairs={{0,16},{4,20},{8,24},{12,28},{16,0},{20,4},{24,8},{28,12},{1,17},{... | collective-permute-start | bytes 196616 | tf_op jit(solution)/shard_map/ppermute | solution.py:383
  99.6 5.5 %collective-permute-start.14 = (f32[128,128]{1,0:T(8,128)S(1)}, f32[128,128]{1,0:T(8,128)S(1)}, u32[]{:S(2)}, u32[]{:S(2)}) collective-permute-start(f32[128,128]{1,0:T(8,128)S(1)} %get-tuple-element.136), channel_id=1, source_target_pairs={{0,12},{4,16},{8,20},{12,24},{16,28},{20,0},{24,4},{28,8},{1,13},{... | collective-permute-start | bytes 196616 | tf_op jit(solution)/shard_map/ppermute | solution.py:383
  101.3 5.5 %collective-permute-start.13 = (f32[128,128]{1,0:T(8,128)S(1)}, f32[128,128]{1,0:T(8,128)S(1)}, u32[]{:S(2)}, u32[]{:S(2)}) collective-permute-start(f32[128,128]{1,0:T(8,128)S(1)} %get-tuple-element.137), channel_id=1, source_target_pairs={{0,8},{4,12},{8,16},{12,20},{16,24},{20,28},{24,0},{28,4},{1,9},{5... | collective-permute-start | bytes 196616 | tf_op jit(solution)/shard_map/ppermute | solution.py:383
  102.5 4.8 %collective-permute-start.12 = (f32[128,128]{1,0:T(8,128)S(1)}, f32[128,128]{1,0:T(8,128)S(1)}, u32[]{:S(2)}, u32[]{:S(2)}) collective-permute-start(f32[128,128]{1,0:T(8,128)S(1)} %get-tuple-element.131), channel_id=1, source_target_pairs={{0,4},{4,8},{8,12},{12,16},{16,20},{20,24},{24,28},{28,0},{1,5},{5... | collective-permute-start | bytes 196616 | tf_op jit(solution)/shard_map/ppermute | solution.py:383
  107.4 16.3 %collective-permute-start.21 = (f32[32,128]{1,0:T(8,128)S(1)}, f32[32,128]{1,0:T(8,128)S(1)}, u32[]{:S(2)}, u32[]{:S(2)}) collective-permute-start(f32[32,128]{1,0:T(8,128)S(1)} %get-tuple-element.139), channel_id=1, source_target_pairs={{0,3},{1,0},{2,1},{3,2},{4,7},{5,4},{6,5},{7,6},{8,11},{9,8},{10,9... | collective-permute-start | bytes 49160 | tf_op jit(solution)/shard_map/ppermute | solution.py:383
  108.7 16.3 %collective-permute-start.20 = (f32[32,128]{1,0:T(8,128)S(1)}, f32[32,128]{1,0:T(8,128)S(1)}, u32[]{:S(2)}, u32[]{:S(2)}) collective-permute-start(f32[32,128]{1,0:T(8,128)S(1)} %get-tuple-element.140), channel_id=1, source_target_pairs={{0,2},{1,3},{2,0},{3,1},{4,6},{5,7},{6,4},{7,5},{8,10},{9,11},{10,... | collective-permute-start | bytes 49160 | tf_op jit(solution)/shard_map/ppermute | solution.py:383
  116.4 10.0 %collective-permute-start.19 = (f32[32,128]{1,0:T(8,128)S(1)}, f32[32,128]{1,0:T(8,128)S(1)}, u32[]{:S(2)}, u32[]{:S(2)}) collective-permute-start(f32[32,128]{1,0:T(8,128)S(1)} %get-tuple-element.138), channel_id=1, source_target_pairs={{0,1},{1,2},{2,3},{3,0},{4,5},{5,6},{6,7},{7,4},{8,9},{9,10},{10,1... | collective-permute-start | bytes 49160 | tf_op jit(solution)/shard_map/ppermute | solution.py:383
  118.3 73.1 %collective-permute-start.6 = (f32[2,1280,128]{2,1,0:T(8,128)}, f32[2,1280,128]{2,1,0:T(8,128)}, u32[]{:S(2)}, u32[]{:S(2)}) collective-permute-start(f32[2,1280,128]{2,1,0:T(8,128)} %get-tuple-element.113), channel_id=1, source_target_pairs={{0,1},{1,2},{2,3},{4,5},{5,6},{6,7},{8,9},{9,10},{10,11},{12,13},{... | collective-permute-start | bytes 3932168 | tf_op jit(solution)/shard_map/ppermute | solution.py:368
  121.3 69.1 %collective-permute-start.7 = (f32[2,1280,128]{2,1,0:T(8,128)}, f32[2,1280,128]{2,1,0:T(8,128)}, u32[]{:S(2)}, u32[]{:S(2)}) collective-permute-start(f32[2,1280,128]{2,1,0:T(8,128)} %get-tuple-element.114), channel_id=1, source_target_pairs={{1,0},{2,1},{3,2},{5,4},{6,5},{7,6},{9,8},{10,9},{11,10},{13,12},{... | collective-permute-start | bytes 3932168 | tf_op jit(solution)/shard_map/ppermute | solution.py:369
  123.6 78.9 %collective-permute-start.8 = (f32[2,128,1024]{2,1,0:T(8,128)}, f32[2,128,1024]{2,1,0:T(8,128)S(1)}, u32[]{:S(2)}, u32[]{:S(2)}) collective-permute-start(f32[2,128,1024]{2,1,0:T(8,128)} %get-tuple-element.115), channel_id=1, source_target_pairs={{0,4},{4,8},{8,12},{12,16},{16,20},{20,24},{24,28},{1,5},{5,9},{9,... | collective-permute-start | bytes 3145736 | tf_op jit(solution)/shard_map/ppermute | solution.py:368
  125.0 79.9 %collective-permute-start.10 = (f32[2,128,1024]{2,1,0:T(8,128)}, f32[2,128,1024]{2,1,0:T(8,128)S(1)}, u32[]{:S(2)}, u32[]{:S(2)}) collective-permute-start(f32[2,128,1024]{2,1,0:T(8,128)} %get-tuple-element.116), channel_id=1, source_target_pairs={{4,0},{8,4},{12,8},{16,12},{20,16},{24,20},{28,24},{5,1},{9,5},{13... | collective-permute-start | bytes 3145736 | tf_op jit(solution)/shard_map/ppermute | solution.py:369
  126.4 27.1 %collective-permute-start.22 = (f32[32,128]{1,0:T(8,128)S(1)}, f32[32,128]{1,0:T(8,128)S(1)}, u32[]{:S(2)}, u32[]{:S(2)}) collective-permute-start(f32[32,128]{1,0:T(8,128)S(1)} %get-tuple-element.120), channel_id=1, source_target_pairs={{0,1},{1,2},{2,3},{3,0},{4,5},{5,6},{6,7},{7,4},{8,9},{9,10},{10,1... | collective-permute-start | bytes 49160 | tf_op jit(solution)/shard_map/ppermute | solution.py:395
  153.4 4.6 %collective-permute-start.23 = (f32[32,128]{1,0:T(8,128)S(1)}, f32[32,128]{1,0:T(8,128)S(1)}, u32[]{:S(2)}, u32[]{:S(2)}) collective-permute-start(f32[32,128]{1,0:T(8,128)S(1)} %get-tuple-element.120), channel_id=1, source_target_pairs={{0,2},{1,3},{2,0},{3,1},{4,6},{5,7},{6,4},{7,5},{8,10},{9,11},{10,... | collective-permute-start | bytes 49160 | tf_op jit(solution)/shard_map/ppermute | solution.py:395
  158.1 3.7 %collective-permute-start.24 = (f32[32,128]{1,0:T(8,128)S(1)}, f32[32,128]{1,0:T(8,128)S(1)}, u32[]{:S(2)}, u32[]{:S(2)}) collective-permute-start(f32[32,128]{1,0:T(8,128)S(1)} %get-tuple-element.120), channel_id=1, source_target_pairs={{0,3},{1,0},{2,1},{3,2},{4,7},{5,4},{6,5},{7,6},{8,11},{9,8},{10,9... | collective-permute-start | bytes 49160 | tf_op jit(solution)/shard_map/ppermute | solution.py:395
  161.8 4.6 %collective-permute-start.25 = (f32[128,128]{1,0:T(8,128)S(1)}, f32[128,128]{1,0:T(8,128)S(1)}, u32[]{:S(2)}, u32[]{:S(2)}) collective-permute-start(f32[128,128]{1,0:T(8,128)S(1)} %constant_dynamic-update-slice_fusion.8), channel_id=1, source_target_pairs={{0,4},{4,8},{8,12},{12,16},{16,20},{20,24},{24,28},{28,0},{1,5},{5... | collective-permute-start | bytes 196616 | tf_op jit(solution)/shard_map/ppermute | solution.py:395
  166.4 5.2 %collective-permute-start.26 = (f32[128,128]{1,0:T(8,128)S(1)}, f32[128,128]{1,0:T(8,128)S(1)}, u32[]{:S(2)}, u32[]{:S(2)}) collective-permute-start(f32[128,128]{1,0:T(8,128)S(1)} %constant_dynamic-update-slice_fusion.8), channel_id=1, source_target_pairs={{0,8},{4,12},{8,16},{12,20},{16,24},{20,28},{24,0},{28,4},{1,9},{5... | collective-permute-start | bytes 196616 | tf_op jit(solution)/shard_map/ppermute | solution.py:395
  171.6 3.7 %collective-permute-start.27 = (f32[128,128]{1,0:T(8,128)S(1)}, f32[128,128]{1,0:T(8,128)S(1)}, u32[]{:S(2)}, u32[]{:S(2)}) collective-permute-start(f32[128,128]{1,0:T(8,128)S(1)} %constant_dynamic-update-slice_fusion.8), channel_id=1, source_target_pairs={{0,12},{4,16},{8,20},{12,24},{16,28},{20,0},{24,4},{28,8},{1,13},{... | collective-permute-start | bytes 196616 | tf_op jit(solution)/shard_map/ppermute | solution.py:395
  175.3 4.3 %collective-permute-start.28 = (f32[128,128]{1,0:T(8,128)S(1)}, f32[128,128]{1,0:T(8,128)S(1)}, u32[]{:S(2)}, u32[]{:S(2)}) collective-permute-start(f32[128,128]{1,0:T(8,128)S(1)} %constant_dynamic-update-slice_fusion.8), channel_id=1, source_target_pairs={{0,16},{4,20},{8,24},{12,28},{16,0},{20,4},{24,8},{28,12},{1,17},{... | collective-permute-start | bytes 196616 | tf_op jit(solution)/shard_map/ppermute | solution.py:395
  179.5 3.7 %collective-permute-start.29 = (f32[128,128]{1,0:T(8,128)S(1)}, f32[128,128]{1,0:T(8,128)S(1)}, u32[]{:S(2)}, u32[]{:S(2)}) collective-permute-start(f32[128,128]{1,0:T(8,128)S(1)} %constant_dynamic-update-slice_fusion.8), channel_id=1, source_target_pairs={{0,20},{4,24},{8,28},{12,0},{16,4},{20,8},{24,12},{28,16},{1,21},{... | collective-permute-start | bytes 196616 | tf_op jit(solution)/shard_map/ppermute | solution.py:395
  183.2 4.3 %collective-permute-start.30 = (f32[128,128]{1,0:T(8,128)S(1)}, f32[128,128]{1,0:T(8,128)S(1)}, u32[]{:S(2)}, u32[]{:S(2)}) collective-permute-start(f32[128,128]{1,0:T(8,128)S(1)} %constant_dynamic-update-slice_fusion.8), channel_id=1, source_target_pairs={{0,24},{4,28},{8,0},{12,4},{16,8},{20,12},{24,16},{28,20},{1,25},{... | collective-permute-start | bytes 196616 | tf_op jit(solution)/shard_map/ppermute | solution.py:395
  187.5 1.9 collective-permute-start.31
  192.4 10.1 %collective-permute-start.9 = (f32[2,2,128,128]{3,2,1,0:T(8,128)S(1)}, f32[2,2,128,128]{3,2,1,0:T(8,128)S(1)}, u32[]{:S(2)}, u32[]{:S(2)}) collective-permute-start(f32[2,2,128,128]{3,2,1,0:T(8,128)S(1)} %pad_maximum_fusion.3), channel_id=1, source_target_pairs={{0,4},{4,8},{8,12},{12,16},{16,20},{20,24},{24,28},{1,5},{5,9},{9,... | collective-permute-start | bytes 786440 | tf_op jit(solution)/shard_map/ppermute | solution.py:368
  195.9 9.0 %collective-permute-start.11 = (f32[2,2,128,128]{3,2,1,0:T(8,128)S(1)}, f32[2,2,128,128]{3,2,1,0:T(8,128)S(1)}, u32[]{:S(2)}, u32[]{:S(2)}) collective-permute-start(f32[2,2,128,128]{3,2,1,0:T(8,128)S(1)} %pad_maximum_fusion.4), channel_id=1, source_target_pairs={{4,0},{8,4},{12,8},{16,12},{20,16},{24,20},{28,24},{5,1},{9,5},{13... | collective-permute-start | bytes 786440 | tf_op jit(solution)/shard_map/ppermute | solution.py:369
